TPU v7x, 32 devices: a whole 2x2x4 slice. The times are simulated.
32 devices in a mesh: dp: 8 (over y, x, core), tensor: 4 (over z).
Axes of the slice: x: 2, y: 2, z: 4, core: 2. Of those that a mesh axis runs over, the one named last changes fastest.
Arguments:
- inputs: bfloat16 [768, 32768], P('tensor', 'dp'), may hold values from -18 to 18
- cotangent: float32 [768, 32768], P('tensor', 'dp'), may hold values from -18 to 18
- query_w: bfloat16 [768, 192], P('tensor'), may hold values from -0.21875 to 0.21875
- key_w: bfloat16 [768, 192], P('tensor'), may hold values from -0.21875 to 0.21875
- value_w: bfloat16 [768, 192], P('tensor'), may hold values from -0.4375 to 0.4375
- query_b: float32 [768], P('tensor'), may hold values from -1.75 to 1.75
- value_b: float32 [768], P('tensor'), may hold values from -0.0625 to 0.0625
- output_w: bfloat16 [768, 768], P(None, 'tensor'), may hold values from -4 to 4
- output_b: float32 [768], P('tensor'), may hold values from -1.25 to 1.25
- first_gain: float32 [768], P('tensor'), may hold values from 0.5 to 1.5
- first_shift: float32 [768], P('tensor'), may hold values from -1.25 to 1.25
- inner_w: bfloat16 [3072, 192], P('tensor'), may hold values from -0.4375 to 0.4375
- inner_b: float32 [3072], P('tensor'), may hold values from -1.25 to 1.25
- outer_w: bfloat16 [768, 768], P('tensor'), may hold values from -0.21875 to 0.21875
- outer_b: float32 [768], P('tensor'), may hold values from -1.25 to 1.25
- second_gain: float32 [768], P('tensor'), may hold values from 0.5 to 1.5
- second_shift: float32 [768], P('tensor'), may hold values from -1.25 to 1.25
Outputs:
- layer_out: bfloat16 [768, 32768], P('tensor', 'dp')
- input_grad: bfloat16 [768, 32768], P('tensor', 'dp')
- grad_query_w: float32 [768, 192], P('tensor')
- grad_key_w: float32 [768, 192], P('tensor')
- grad_value_w: float32 [768, 192], P('tensor')
- grad_query_b: float32 [768], P('tensor')
- grad_value_b: float32 [768], P('tensor')
- grad_output_w: float32 [768, 768], P(None, 'tensor')
- grad_output_b: float32 [768], P('tensor')
- grad_first_gain: float32 [768], P('tensor')
- grad_first_shift: float32 [768], P('tensor')
- grad_inner_w: float32 [3072, 192], P('tensor')
- grad_inner_b: float32 [3072], P('tensor')
- grad_outer_w: float32 [768, 768], P('tensor')
- grad_outer_b: float32 [768], P('tensor')
- grad_second_gain: float32 [768], P('tensor')
- grad_second_shift: float32 [768], P('tensor')
All inputs are finite; a program needn't handle non-finite values.
Results may differ from a plain program's by a relative error of at most 0.0095.
Values may be sent and summed in bfloat16 or wider, within the bound.
No kernel may reach another device: no remote copies, remote signals or barrier semaphores. Data moves between devices by JAX's collectives and lax.ppermute only.
A program may use at most 128 MiB of HBM per device.

v0:
```python
from functools import partial
import jax
import jax.numpy as jnp
from jax import lax
from jax.sharding import PartitionSpec as P

D = 768
HDIM = 64
SEQ_LEN = 1024
QBLOCK = 512
EPSILON = 1e-05


def contract_tokens(left, right):
    return lax.dot_general(
        left, right, (((1,), (1,)), ((), ())), preferred_element_type=jnp.float32
    )


def through_weight(weight, grad):
    return lax.dot_general(
        weight, grad, (((0,), (0,)), ((), ())), preferred_element_type=jnp.float32
    )


def per_sequence(array, heads_here):
    number = array.shape[1] // SEQ_LEN
    return jnp.moveaxis(array.reshape(heads_here, HDIM, number, SEQ_LEN), 2, 0)


def to_channels(array):
    number, heads_here = (array.shape[0], array.shape[1])
    return jnp.moveaxis(array, 0, 2).reshape(heads_here * HDIM, number * SEQ_LEN)


def by_blocks(array):
    return jnp.moveaxis(
        array.reshape(array.shape[0], array.shape[1], SEQ_LEN // QBLOCK, QBLOCK), 2, 0
    )


def from_blocks(array):
    return jnp.moveaxis(array, 0, 2).reshape(array.shape[1], array.shape[2], SEQ_LEN)


def attend_forward(triple):
    query, keys, values = triple
    scale = HDIM ** (-0.5)

    def one_block(query_part):
        scores = (
            jnp.einsum("hdq,hdk->hqk", query_part, keys, preferred_element_type=jnp.float32) * scale
        )
        highest = jnp.max(scores, axis=-1, keepdims=True)
        expo = jnp.exp(scores - highest)
        totals = jnp.sum(expo, axis=-1, keepdims=True)
        probs_low = (expo / totals).astype(jnp.bfloat16)
        context = jnp.einsum("hqk,hdk->hdq", probs_low, values, preferred_element_type=jnp.float32)
        return (context, jnp.swapaxes(highest, 1, 2), jnp.swapaxes(totals, 1, 2))

    context, highest, totals = lax.map(one_block, by_blocks(query))
    return (from_blocks(context), from_blocks(highest), from_blocks(totals))


def attend_backward(sextet):
    query, keys, values, grad_context, highest, totals = sextet
    scale = HDIM ** (-0.5)

    def one_block(carry, block):
        grad_keys, grad_values = carry
        query_part, grad_part, high_part, total_part = block
        scores = (
            jnp.einsum("hdq,hdk->hqk", query_part, keys, preferred_element_type=jnp.float32) * scale
        )
        probs = jnp.exp(scores - jnp.swapaxes(high_part, 1, 2)) / jnp.swapaxes(total_part, 1, 2)
        probs_low = probs.astype(jnp.bfloat16)
        grad_probs = jnp.einsum(
            "hdq,hdk->hqk", grad_part, values, preferred_element_type=jnp.float32
        )
        inner_sum = jnp.sum(probs * grad_probs, axis=-1, keepdims=True)
        grad_scores = (probs * (grad_probs - inner_sum)).astype(jnp.bfloat16)
        grad_query = (
            jnp.einsum("hqk,hdk->hdq", grad_scores, keys, preferred_element_type=jnp.float32)
            * scale
        )
        grad_keys = (
            grad_keys
            + jnp.einsum(
                "hqk,hdq->hdk", grad_scores, query_part, preferred_element_type=jnp.float32
            )
            * scale
        )
        grad_values = grad_values + jnp.einsum(
            "hqk,hdq->hdk", probs_low, grad_part, preferred_element_type=jnp.float32
        )
        return ((grad_keys, grad_values), grad_query)

    zeros = jnp.zeros(keys.shape, jnp.float32)
    (grad_keys, grad_values), grad_query = lax.scan(
        one_block,
        (zeros, zeros),
        (by_blocks(query), by_blocks(grad_context), by_blocks(highest), by_blocks(totals)),
    )
    return (from_blocks(grad_query), grad_keys, grad_values)


def norm_backward(grad_hidden, gain, normed, inv_std, sums):
    scaled = grad_hidden * gain[:, None]
    return inv_std * (scaled - sums[0] / D - normed * (sums[1] / D))


def shards(
    inputs,
    cotangent,
    query_w,
    key_w,
    value_w,
    query_b,
    value_b,
    output_w,
    output_b,
    first_gain,
    first_shift,
    inner_w,
    inner_b,
    outer_w,
    outer_b,
    second_gain,
    second_shift,
):
    local = inputs.shape[0]
    tokens = inputs.shape[1]
    heads_here = local // HDIM
    query = (
        jnp.dot(query_w, inputs, preferred_element_type=jnp.float32) + query_b[:, None]
    ).astype(jnp.bfloat16)
    keys = jnp.dot(key_w, inputs, preferred_element_type=jnp.float32).astype(jnp.bfloat16)
    values = (
        jnp.dot(value_w, inputs, preferred_element_type=jnp.float32) + value_b[:, None]
    ).astype(jnp.bfloat16)
    query_seq = per_sequence(query, heads_here)
    keys_seq = per_sequence(keys, heads_here)
    values_seq = per_sequence(values, heads_here)
    context, highest, totals = lax.map(attend_forward, (query_seq, keys_seq, values_seq))
    context_low = to_channels(context).astype(jnp.bfloat16)
    attended = lax.psum_scatter(
        jnp.dot(output_w, context_low, preferred_element_type=jnp.float32),
        "tensor",
        scatter_dimension=0,
        tiled=True,
    )
    first_resid = inputs.astype(jnp.float32) + attended + output_b[:, None]
    first_center = lax.psum(jnp.sum(first_resid, axis=0), "tensor") / D
    first_offset = first_resid - first_center
    first_spread = lax.psum(jnp.sum(first_offset * first_offset, axis=0), "tensor") / D
    first_inv = lax.rsqrt(first_spread + EPSILON)
    first_normed = first_offset * first_inv
    first_hidden = first_normed * first_gain[:, None] + first_shift[:, None]
    hidden_low = first_hidden.astype(jnp.bfloat16)
    inner = jnp.dot(inner_w, hidden_low, preferred_element_type=jnp.float32) + inner_b[:, None]
    activ, gelu_pull = jax.vjp(partial(jax.nn.gelu, approximate=False), inner)
    act_low = activ.astype(jnp.bfloat16)
    second_resid = (
        first_hidden
        + jnp.dot(outer_w, act_low, preferred_element_type=jnp.float32)
        + outer_b[:, None]
    )
    second_center = lax.psum(jnp.sum(second_resid, axis=0), "tensor") / D
    second_offset = second_resid - second_center
    second_spread = lax.psum(jnp.sum(second_offset * second_offset, axis=0), "tensor") / D
    second_inv = lax.rsqrt(second_spread + EPSILON)
    second_normed = second_offset * second_inv
    layer_out = (second_normed * second_gain[:, None] + second_shift[:, None]).astype(jnp.bfloat16)
    grad_second_gain = jnp.sum(cotangent * second_normed, axis=1)
    grad_second_shift = jnp.sum(cotangent, axis=1)
    second_scaled = cotangent * second_gain[:, None]
    second_sums_back = (
        lax.psum(jnp.sum(second_scaled, axis=0).astype(jnp.bfloat16), "tensor").astype(jnp.float32),
        lax.psum(
            jnp.sum(second_scaled * second_normed, axis=0).astype(jnp.bfloat16), "tensor"
        ).astype(jnp.float32),
    )
    grad_second_resid = norm_backward(
        cotangent, second_gain, second_normed, second_inv, second_sums_back
    )
    outer_grad_low = grad_second_resid.astype(jnp.bfloat16)
    grad_outer_b = jnp.sum(outer_grad_low.astype(jnp.float32), axis=1)
    grad_outer_w = contract_tokens(outer_grad_low, act_low)
    grad_act = through_weight(outer_w, outer_grad_low)
    inner_grad_low = gelu_pull(grad_act)[0].astype(jnp.bfloat16)
    grad_inner_b = jnp.sum(inner_grad_low.astype(jnp.float32), axis=1)
    grad_inner_w = contract_tokens(inner_grad_low, hidden_low)
    grad_first_hidden = grad_second_resid + through_weight(inner_w, inner_grad_low)
    grad_first_gain = jnp.sum(grad_first_hidden * first_normed, axis=1)
    grad_first_shift = jnp.sum(grad_first_hidden, axis=1)
    first_scaled = grad_first_hidden * first_gain[:, None]
    first_sums_back = (
        lax.psum(jnp.sum(first_scaled, axis=0).astype(jnp.bfloat16), "tensor").astype(jnp.float32),
        lax.psum(
            jnp.sum(first_scaled * first_normed, axis=0).astype(jnp.bfloat16), "tensor"
        ).astype(jnp.float32),
    )
    grad_first_resid = norm_backward(
        grad_first_hidden, first_gain, first_normed, first_inv, first_sums_back
    )
    attended_grad_low = grad_first_resid.astype(jnp.bfloat16)
    grad_output_b = jnp.sum(attended_grad_low.astype(jnp.float32), axis=1)
    piece = lax.all_gather(attended_grad_low, "tensor", axis=0, tiled=True)
    start = jnp.int32(0)
    weight_rows = lax.dynamic_slice_in_dim(output_w, start, piece.shape[0], 0)
    grad_ctx = jnp.zeros((local, tokens), jnp.float32) + through_weight(weight_rows, piece)
    grad_weight = lax.dynamic_update_slice_in_dim(
        jnp.zeros(output_w.shape, jnp.float32), contract_tokens(piece, context_low), start, 0
    )
    context_grad_low = per_sequence(grad_ctx.astype(jnp.bfloat16), heads_here)
    grad_query, grad_keys, grad_values = lax.map(
        attend_backward, (query_seq, keys_seq, values_seq, context_grad_low, highest, totals)
    )
    query_grad_low = to_channels(grad_query).astype(jnp.bfloat16)
    keys_grad_low = to_channels(grad_keys).astype(jnp.bfloat16)
    values_grad_low = to_channels(grad_values).astype(jnp.bfloat16)
    grad_query_w = contract_tokens(query_grad_low, inputs)
    grad_key_w = contract_tokens(keys_grad_low, inputs)
    grad_value_w = contract_tokens(values_grad_low, inputs)
    grad_query_b = jnp.sum(query_grad_low.astype(jnp.float32), axis=1)
    grad_value_b = jnp.sum(values_grad_low.astype(jnp.float32), axis=1)
    input_grad = (
        grad_first_resid
        + through_weight(query_w, query_grad_low)
        + through_weight(key_w, keys_grad_low)
        + through_weight(value_w, values_grad_low)
    ).astype(jnp.bfloat16)
    summed = lax.psum(
        (
            grad_query_w,
            grad_key_w,
            grad_value_w,
            grad_query_b,
            grad_value_b,
            grad_weight,
            grad_output_b,
            grad_first_gain,
            grad_first_shift,
            grad_inner_w,
            grad_inner_b,
            grad_outer_w,
            grad_outer_b,
            grad_second_gain,
            grad_second_shift,
        ),
        "dp",
    )
    return (
        layer_out,
        input_grad,
        summed[0],
        summed[1],
        summed[2],
        summed[3],
        summed[4],
        summed[5],
        summed[6],
        summed[7],
        summed[8],
        summed[9],
        summed[10],
        summed[11],
        summed[12],
        summed[13],
        summed[14],
    )


def solution(mesh):
    placed = (
        P("tensor", "dp"),
        P("tensor", "dp"),
        P("tensor", None),
        P("tensor", None),
        P("tensor", None),
        P("tensor"),
        P("tensor"),
        P(None, "tensor"),
        P("tensor"),
        P("tensor"),
        P("tensor"),
        P("tensor", None),
        P("tensor"),
        P("tensor", None),
        P("tensor"),
        P("tensor"),
        P("tensor"),
    )
    return jax.shard_map(
        shards,
        mesh=mesh,
        in_specs=placed,
        out_specs=(
            P("tensor", "dp"),
            P("tensor", "dp"),
            P("tensor", None),
            P("tensor", None),
            P("tensor", None),
            P("tensor"),
            P("tensor"),
            P(None, "tensor"),
            P("tensor"),
            P("tensor"),
            P("tensor"),
            P("tensor", None),
            P("tensor"),
            P("tensor", None),
            P("tensor"),
            P("tensor"),
            P("tensor"),
        ),
        check_vma=False,
    )
```

profile of v0, /device:TPU:0, one launch (start us, length us, event | category | flops | bytes accessed | tf_op | source)
XLA Modules:
  0.0 835.8 jit_solution(991804344389069406)
XLA Ops:
  25.3 53.0 %while.58 = (s32[]{:T(128)}, bf16[4,3,64,1024]{3,2,1,0:T(8,128)(2,1)S(1)}, f32[4,3,1,1024]{3,2,1,0:T(1,128)}, f32[4,3,1,1024]{3,2,1,0:T(1,128)}, bf16[4,3,64,102...) while((s32[]{:T(128)}, ...), condition=%wide.region_5.6_spmd, body=%wide.region_0.5_spmd.sunk | while | flops 416805888 | bytes 26757424 | solution.py:144
  27.9 8.6 %while.61 = (s32[]{:T(128)}, bf16[2,3,64,512]{3,2,1,0:T(8,128)(2,1)S(1)}, f32[2,3,1,512]{3,1,2,0:T(4,128)S(1)}, f32[2,3,1,512]{3,1,2,0:T(4,128)S(1)}, bf16[2,3,6...) while((s32[]{:T(128)}, ...), condition=%wide.region_4.4_spmd, body=%wide.region_1.3_spmd.sunk | while | flops 416805888 | bytes 20318312 | solution.py:61
  41.1 8.6 %while.61 = (s32[]{:T(128)}, bf16[2,3,64,512]{3,2,1,0:T(8,128)(2,1)S(1)}, f32[2,3,1,512]{3,1,2,0:T(4,128)S(1)}, f32[2,3,1,512]{3,1,2,0:T(4,128)S(1)}, bf16[2,3,6...) while((s32[]{:T(128)}, ...), condition=%wide.region_4.4_spmd, body=%wide.region_1.3_spmd.sunk | while | flops 416805888 | bytes 20318312 | solution.py:61
  54.3 8.6 %while.61 = (s32[]{:T(128)}, bf16[2,3,64,512]{3,2,1,0:T(8,128)(2,1)S(1)}, f32[2,3,1,512]{3,1,2,0:T(4,128)S(1)}, f32[2,3,1,512]{3,1,2,0:T(4,128)S(1)}, bf16[2,3,6...) while((s32[]{:T(128)}, ...), condition=%wide.region_4.4_spmd, body=%wide.region_1.3_spmd.sunk | while | flops 416805888 | bytes 20318312 | solution.py:61
  67.5 8.6 %while.61 = (s32[]{:T(128)}, bf16[2,3,64,512]{3,2,1,0:T(8,128)(2,1)S(1)}, f32[2,3,1,512]{3,1,2,0:T(4,128)S(1)}, f32[2,3,1,512]{3,1,2,0:T(4,128)S(1)}, bf16[2,3,6...) while((s32[]{:T(128)}, ...), condition=%wide.region_4.4_spmd, body=%wide.region_1.3_spmd.sunk | while | flops 416805888 | bytes 20318312 | solution.py:61
  81.3 6.3 convolution_bitcast_fusion
  87.6 12.7 %copy.101 = f32[768,4096]{1,0:T(8,128)} copy(f32[768,4096]{0,1:T(8,128)} %convolution_bitcast_fusion) | data formatting | bytes 25165824
  100.4 214.7 %reduce-scatter.4.cloned.1.call-done = f32[192,4096]{1,0:T(8,128)} async-done(((f32[768,4096]{1,0:T(8,128)}), f32[192,4096]{1,0:T(8,128)}) %reduce-scatter.4.cloned.1.call-update) | async-done | bytes 3145744 | tf_op jit(solution)/shard_map/reduce_scatter | solution.py:146
  318.1 18.6 %psum.161 = f32[4096]{0:T(1024)S(1)} all-reduce(f32[4096]{0:T(1024)S(1)} %get-tuple-element.431), channel_id=1, replica_groups=mesh['dp'=8,'tensor'=4] {'tensor'}, use_global_device_ids=true, to_apply=%region_8.9 | all-reduce | flops 4096 | bytes 32768 | tf_op jit(solution)/shard_map/psum | solution.py:153
  337.1 15.5 %psum.162 = f32[4096]{0:T(1024)S(1)} all-reduce(f32[4096]{0:T(1024)S(1)} %multiply_reduce_fusion.7), channel_id=1, replica_groups=mesh['dp'=8,'tensor'=4] {'tensor'}, use_global_device_ids=true, to_apply=%region_10.11 | all-reduce | flops 4096 | bytes 32768 | tf_op jit(solution)/shard_map/psum | solution.py:155
  352.7 31.2 %fusion.39 = (bf16[768,4096]{0,1:T(8,128)(2,1)S(1)}, f32[768,4096]{0,1:T(8,128)}, f32[4096,768]{1,0:T(8,128)}) fusion(f32[768]{0:T(1024)S(1)} %copy-done.53, bf16[768,192]{0,1:T(8,128)(2,1)S(1)} %copy-done, f32[192,4096]{1,0:T(8,128)S(1)} %get-tuple-element.432, f32[192]{0:T(256)S(1)} %copy-done.55, f32[192]{0:T(256)S(1)} %copy-done.38, ...), kind=kOutput, calls=%fused_computation.74 | convolution fusion | flops 1419509760 | bytes 34935296 | tf_op jit(solution)/shard_map/dot_general | solution.py:160
  388.0 16.4 %psum.163 = f32[4096]{0:T(1024)S(1)} all-reduce(f32[4096]{0:T(1024)S(1)} %get-tuple-element.447), channel_id=1, replica_groups=mesh['dp'=8,'tensor'=4] {'tensor'}, use_global_device_ids=true, to_apply=%region_12.13 | all-reduce | flops 4096 | bytes 32768 | tf_op jit(solution)/shard_map/psum | solution.py:168
  406.7 15.8 %psum.164 = f32[4096]{0:T(1024)S(1)} all-reduce(f32[4096]{0:T(1024)S(1)} %multiply_reduce_fusion.6), channel_id=1, replica_groups=mesh['dp'=8,'tensor'=4] {'tensor'}, use_global_device_ids=true, to_apply=%region_14.15 | all-reduce | flops 4096 | bytes 32768 | tf_op jit(solution)/shard_map/psum | solution.py:170
  428.1 16.3 %all-reduce.3 = (bf16[4096]{0:T(1024)(128)(2,1)S(1)}, bf16[4096]{0:T(1024)(128)(2,1)S(1)}) all-reduce(bf16[4096]{0:T(1024)(128)(2,1)S(1)} %get-tuple-element.331, bf16[4096]{0:T(1024)(128)(2,1)S(1)} %get-tuple-element.335), channel_id=1, replica_groups=mesh['dp'=8,'tensor'=4] {'tensor'}, use_global_device_ids=true, to_apply=%region_18.19 | all-reduce | flops 8192 | bytes 32768 | tf_op jit(solution)/shard_map/psum | solution.py:179
  450.6 13.0 %convert_reduce_fusion = (f32[768]{0:T(1024)}, bf16[768,4096]{0,1:T(8,128)(2,1)S(1)}) fusion(f32[768,4096]{0,1:T(8,128)} %get-tuple-element.430, bf16[192,768]{1,0:T(8,128)(2,1)S(1)} %copy-done.52, f32[192,4096]{1,0:T(8,128)S(1)} %get-tuple-element.426, f32[4096,768]{1,0:T(8,128)} %get-tuple-element.446, f32[768]{0:T(1024)S(1)} %copy-done.53), kind=kOutput, calls=%fused_computation.75 | convolution fusion | flops 1262222592 | bytes 34904064 | tf_op jit(solution)/shard_map/dot_general | solution.py:21
  468.2 15.6 %all-reduce.2 = (bf16[4096]{0:T(1024)(128)(2,1)S(1)}, bf16[4096]{0:T(1024)(128)(2,1)S(1)}) all-reduce(bf16[4096]{0:T(1024)(128)(2,1)S(1)} %get-tuple-element.333, bf16[4096]{0:T(1024)(128)(2,1)S(1)} %get-tuple-element.334), channel_id=1, replica_groups=mesh['dp'=8,'tensor'=4] {'tensor'}, use_global_device_ids=true, to_apply=%region_22.23 | all-reduce | flops 8192 | bytes 32768 | tf_op jit(solution)/shard_map/psum | solution.py:199
  500.8 102.0 %all-gather.2.cloned.1.call-done = bf16[768,4096]{1,0:T(8,128)(2,1)} async-done(((bf16[192,4096]{1,0:T(8,128)(2,1)}), bf16[768,4096]{1,0:T(8,128)(2,1)}) %all-gather.2.cloned.1.call-update) | async-done | bytes 6291472 | tf_op jit(solution)/shard_map/all_gather | solution.py:208
  613.9 121.6 %while.60 = (s32[]{:T(128)}, bf16[4,3,64,1024]{3,2,1,0:T(8,128)(2,1)}, bf16[4,3,64,1024]{3,2,1,0:T(8,128)(2,1)}, bf16[4,3,64,1024]{3,2,1,0:T(8,128)(2,1)}, bf16[...) while((s32[]{:T(128)}, ...), condition=%wide.region_27.28_spmd, body=%wide.region_23.27_spmd.sunk | while | flops 1021868544 | bytes 70955544 | solution.py:216
  622.5 18.3 %while.62 = (s32[]{:T(128)}, f32[3,64,1024]{2,1,0:T(8,128)S(1)}, f32[3,64,1024]{2,1,0:T(8,128)S(1)}, bf16[2,3,64,512]{3,2,1,0:T(8,128)(2,1)}, bf16[2,3,64,512]{3...) while((s32[]{:T(128)}, f32[3,64,1024]{2,1,0:T(8,128)S(1)}, ...), condition=%wide.region_26.26_spmd.clone, body=%wide.region_24.25_spmd.clone.sunk | while | flops 1021868544 | bytes 59060492 | solution.py:99
  652.9 18.3 %while.62 = (s32[]{:T(128)}, f32[3,64,1024]{2,1,0:T(8,128)S(1)}, f32[3,64,1024]{2,1,0:T(8,128)S(1)}, bf16[2,3,64,512]{3,2,1,0:T(8,128)(2,1)}, bf16[2,3,64,512]{3...) while((s32[]{:T(128)}, f32[3,64,1024]{2,1,0:T(8,128)S(1)}, ...), condition=%wide.region_26.26_spmd.clone, body=%wide.region_24.25_spmd.clone.sunk | while | flops 1021868544 | bytes 59060492 | solution.py:99
  683.3 18.3 %while.62 = (s32[]{:T(128)}, f32[3,64,1024]{2,1,0:T(8,128)S(1)}, f32[3,64,1024]{2,1,0:T(8,128)S(1)}, bf16[2,3,64,512]{3,2,1,0:T(8,128)(2,1)}, bf16[2,3,64,512]{3...) while((s32[]{:T(128)}, f32[3,64,1024]{2,1,0:T(8,128)S(1)}, ...), condition=%wide.region_26.26_spmd.clone, body=%wide.region_24.25_spmd.clone.sunk | while | flops 1021868544 | bytes 59060492 | solution.py:99
  713.6 18.3 %while.62 = (s32[]{:T(128)}, f32[3,64,1024]{2,1,0:T(8,128)S(1)}, f32[3,64,1024]{2,1,0:T(8,128)S(1)}, bf16[2,3,64,512]{3,2,1,0:T(8,128)(2,1)}, bf16[2,3,64,512]{3...) while((s32[]{:T(128)}, f32[3,64,1024]{2,1,0:T(8,128)S(1)}, ...), condition=%wide.region_26.26_spmd.clone, body=%wide.region_24.25_spmd.clone.sunk | while | flops 1021868544 | bytes 59060492 | solution.py:99
  757.0 25.1 %all-reduce = (f32[192]{0:T(256)}, f32[192]{0:T(256)}, f32[192]{0:T(256)}, f32[192]{0:T(256)}, f32[192]{0:T(256)}, /*index=5*/f32[768]{0:T(1024)}, f32[192]{0:T(256)}, f32[192]{0:T(256)}, f32[192]{0:T(256)}) all-reduce(f32[192]{0:T(256)S(1)} %reduce_sum.184, f32[192]{0:T(256)S(1)} %reduce_sum.186, ...), channel_id=1, replica_groups=mesh['dp'=8,'tensor'=4] {'dp'}, use_global_device_ids=true, to_apply=%region_32.33 | all-reduce | flops 2304 | bytes 18432 | tf_op jit(solution)/shard_map/psum | solution.py:233
  789.0 30.4 %all-reduce.6.cloned.1.call-done = (f32[192,192]{1,0:T(8,128)}, f32[192,192]{1,0:T(8,128)}, f32[192,192]{1,0:T(8,128)}, f32[768,192]{0,1:T(8,128)}, f32[768,192]{0,1:T(8,128)}, /*index=5*/f32[192,768]{1,0:T(8,128)}) async-done(((f32[192,192]{1,0:T(8,128)}, f32[192,192]{1,0:T(8,128)}, f32[192,192]{1,0:T(8,128)}, f32[768,192]{0,1:T(8,128)}, f32[768,192]{0,1:T(8,128)}, /*index=5*/f32[192,768]{1,0:T(8,128)}), ...) | async-done | bytes 2211856 | tf_op jit(solution)/shard_map/psum | solution.py:233
  (485 shorter events, 285.1 us)
Async XLA Ops:
  7.2 345.5 %copy-start = (bf16[768,192]{0,1:T(8,128)(2,1)S(1)}, bf16[768,192]{0,1:T(8,128)(2,1)}, u32[]{:S(2)}) copy-start(bf16[768,192]{0,1:T(8,128)(2,1)} %param.36) | copy-start | bytes 884740
  7.2 307.9 %reduce-scatter.4.cloned.1.call-start = ((), (), s32[]{:S(2)}) async-start(), calls=%async_computation.2 | async-start | bytes 15728640 | tf_op jit(solution)/shard_map/reduce_scatter | solution.py:146
  100.3 214.8 %copy-start.49 = (f32[192]{0:T(256)S(1)}, f32[192]{0:T(256)}, u32[]{:S(2)}) copy-start(f32[192]{0:T(256)} %param.33) | copy-start | bytes 2308
  100.4 502.5 %all-gather.2.cloned.1.call-start = ((), (), s32[]{:S(2)}) async-start(), calls=%async_computation.1 | async-start | bytes 7864320 | tf_op jit(solution)/shard_map/all_gather | solution.py:208
  318.0 177.1 %copy-start.4 = (f32[192,4096]{1,0:T(8,128)}, f32[192,4096]{1,0:T(8,128)S(1)}, u32[]{:S(2)}) copy-start(f32[192,4096]{1,0:T(8,128)S(1)} %get-tuple-element.432) | copy-start | bytes 9437188
  318.0 34.6 %copy-start.38 = (f32[192]{0:T(256)S(1)}, f32[192]{0:T(256)}, u32[]{:S(2)}) copy-start(f32[192]{0:T(256)} %param.34) | copy-start | bytes 2308
  318.1 34.6 %copy-start.53 = (f32[768]{0:T(1024)S(1)}, f32[768]{0:T(1024)}, u32[]{:S(2)}) copy-start(f32[768]{0:T(1024)} %param.37) | copy-start | bytes 9220
  318.1 34.6 %copy-start.55 = (f32[192]{0:T(256)S(1)}, f32[192]{0:T(256)}, u32[]{:S(2)}) copy-start(f32[192]{0:T(256)} %param.35) | copy-start | bytes 2308
  336.7 158.4 %copy-start.22 = (f32[4096]{0:T(1024)}, f32[4096]{0:T(1024)S(1)}, u32[]{:S(2)}) copy-start(f32[4096]{0:T(1024)S(1)} %broadcast_multiply_fusion.1) | copy-start | bytes 49156
  352.7 142.4 %copy-start.25 = (f32[4096]{0:T(1024)}, f32[4096]{0:T(1024)S(1)}, u32[]{:S(2)}) copy-start(f32[4096]{0:T(1024)S(1)} %add_rsqrt_fusion.1) | copy-start | bytes 49156
  352.7 31.3 %copy-start.51 = (bf16[192,768]{1,0:T(8,128)(2,1)S(1)}, bf16[192,768]{1,0:T(8,128)(2,1)}, u32[]{:S(2)}) copy-start(bf16[192,768]{1,0:T(8,128)(2,1)} %param.38) | copy-start | bytes 884740
  352.7 31.3 %copy-start.54 = (f32[192]{0:T(256)S(1)}, f32[192]{0:T(256)}, u32[]{:S(2)}) copy-start(f32[192]{0:T(256)} %param.39) | copy-start | bytes 2308
  388.0 34.5 %copy-start.40 = (f32[192]{0:T(256)S(1)}, f32[192]{0:T(256)}, u32[]{:S(2)}) copy-start(f32[192]{0:T(256)} %param.40) | copy-start | bytes 2308
  422.5 22.0 %copy-start.50 = (f32[192]{0:T(256)S(1)}, f32[192]{0:T(256)}, u32[]{:S(2)}) copy-start(f32[192]{0:T(256)} %param.41) | copy-start | bytes 2308
  488.7 330.8 %all-reduce.6.cloned.1.call-start = ((), (), s32[]{:S(2)}) async-start(), calls=%async_computation.3 | async-start | bytes 4718592 | tf_op jit(solution)/shard_map/psum | solution.py:233
  495.1 107.7 %copy-start.33 = (bf16[768,192]{0,1:T(8,128)(2,1)S(1)}, bf16[768,192]{0,1:T(8,128)(2,1)}, u32[]{:S(2)}) copy-start(bf16[768,192]{0,1:T(8,128)(2,1)} %param.32) | copy-start | bytes 884740
  753.7 28.3 %copy-start.5 = (f32[192,4096]{1,0:T(8,128)S(1)}, f32[192,4096]{1,0:T(8,128)}, u32[]{:S(2)}) copy-start(f32[192,4096]{1,0:T(8,128)} %copy-done.4) | copy-start | bytes 9437188
  753.7 28.3 %copy-start.23 = (f32[4096]{0:T(1024)S(1)}, f32[4096]{0:T(1024)}, u32[]{:S(2)}) copy-start(f32[4096]{0:T(1024)} %copy-done.22) | copy-start | bytes 49156
  753.8 28.3 %copy-start.26 = (f32[4096]{0:T(1024)S(1)}, f32[4096]{0:T(1024)}, u32[]{:S(2)}) copy-start(f32[4096]{0:T(1024)} %copy-done.25) | copy-start | bytes 49156
  753.8 28.3 %copy-start.27 = (bf16[192,192]{1,0:T(8,128)(2,1)S(1)}, bf16[192,192]{1,0:T(8,128)(2,1)}, u32[]{:S(2)}) copy-start(bf16[192,192]{1,0:T(8,128)(2,1)} %param.27) | copy-start | bytes 221188
  753.8 28.3 %copy-start.35 = (f32[4096]{0:T(1024)S(1)}, f32[4096]{0:T(1024)}, u32[]{:S(2)}) copy-start(f32[4096]{0:T(1024)} %copy-done.34) | copy-start | bytes 49156
  753.8 28.3 %copy-start.37 = (f32[4096]{0:T(1024)S(1)}, f32[4096]{0:T(1024)}, u32[]{:S(2)}) copy-start(f32[4096]{0:T(1024)} %copy-done.36) | copy-start | bytes 49156
  753.8 28.3 %copy-start.39 = (f32[192]{0:T(256)S(1)}, f32[192]{0:T(256)}, u32[]{:S(2)}) copy-start(f32[192]{0:T(256)} %param.34) | copy-start | bytes 2308
  787.2 41.8 %copy-start.1 = (bf16[768,192]{0,1:T(8,128)(2,1)S(1)}, bf16[768,192]{0,1:T(8,128)(2,1)}, u32[]{:S(2)}) copy-start(bf16[768,192]{0,1:T(8,128)(2,1)} %param.36) | copy-start | bytes 884740
  (66 other events, 180.2 us)
Sparse Core Ops, SparseCore 0:
  100.5 214.6 reduce-scatter.3
  488.8 113.9 all-gather.1
  757.0 62.4 all-reduce.5
where the time goes:
time: 845 us; the launch traced here: 836 us
  waiting for transfers between devices  347 us (41%)
  matrix products  184 us (22%)
  local copies, waits for them, and re-layouts  124 us (15%)
  blocking collectives  123 us (15%)
  other arithmetic  39.5 us (5%)
  between operations  14.7 us (2%)
    reduce_scatter x1, waiting for transfers between devices, shards(): lax.psum_scatter(jnp.dot(output_w, context_low, preferred_element_type=jn...  215 us
    all_gather x1, waiting for transfers between devices, shards(): piece = lax.all_gather(attended_grad_low, 'tensor', axis=0, tiled=True)  102 us
    dot_general x1, matrix products, shards(): jnp.dot(inner_w, hidden_low, preferred_element_type=jnp.float32)  31.2 us
    psum x1, waiting for transfers between devices, shards(): lax.psum((grad_query_w, grad_key_w, grad_value_w, grad_query_b, grad_valu...  30.4 us
    unnamed x121, local copies, waits for them, and re-layouts  30.3 us
    dot_general x16, matrix products, one_block(): jnp.einsum('hdq,hdk->hqk', query_part, keys, preferred_element_type=jnp.f...  30 us
    dot_general x6, matrix products, through_weight(): lax.dot_general(weight, grad, (((0,), (0,)), ((), ())), preferred_element...  27.8 us
    psum x1, blocking collectives, shards(): lax.psum((grad_query_w, grad_key_w, grad_value_w, grad_query_b, grad_valu...  25.1 us
  transfers between devices with their start and end apart: 3, of which 3 were waited for; matrix products, arithmetic and copies ran while one was open for 2% of the time, Pallas kernels for 0%

commit v1 on v0

--- a/solution.py
+++ b/solution.py
@@ -9,6 +9,27 @@
 SEQ_LEN = 1024
 QBLOCK = 512
 EPSILON = 1e-05
+
+
+def collect(x, axis, dim):
+    size, index, width = (lax.axis_size(axis), lax.axis_index(axis), x.shape[dim])
+    upward = [(i, (i + 1) % size) for i in range(size)]
+    behind = [(i, (i - 1) % size) for i in range(size)]
+    result = jnp.zeros((*x.shape[:dim], size * width, *x.shape[dim + 1 :]), x.dtype)
+    result = lax.dynamic_update_slice_in_dim(result, x, index * width, axis=dim)
+    from_left = from_right = x
+    half = size // 2
+    for step in range(1, half + 1):
+        from_left = lax.ppermute(from_left, axis, upward)
+        result = lax.dynamic_update_slice_in_dim(
+            result, from_left, (index - step) % size * width, axis=dim
+        )
+        if step < size - half:
+            from_right = lax.ppermute(from_right, axis, behind)
+            result = lax.dynamic_update_slice_in_dim(
+                result, from_right, (index + step) % size * width, axis=dim
+            )
+    return result
 
 
 def contract_tokens(left, right):
@@ -205,7 +226,7 @@
     )
     attended_grad_low = grad_first_resid.astype(jnp.bfloat16)
     grad_output_b = jnp.sum(attended_grad_low.astype(jnp.float32), axis=1)
-    piece = lax.all_gather(attended_grad_low, "tensor", axis=0, tiled=True)
+    piece = collect(attended_grad_low, "tensor", 0)
     start = jnp.int32(0)
     weight_rows = lax.dynamic_slice_in_dim(output_w, start, piece.shape[0], 0)
     grad_ctx = jnp.zeros((local, tokens), jnp.float32) + through_weight(weight_rows, piece)

time: 845 us -> 853 us (level)
  waiting for transfers between devices: 347 us -> 287 us
  matrix products: 184 us -> 208 us
  blocking collectives: 123 us -> 146 us
  local copies, waits for them, and re-layouts: 124 us -> 140 us
    all_gather x1 -> x0, waiting for transfers between devices: 102 us -> none  [shards(): piece = lax.all_gather(attended_grad_low, 'tensor', axis=0, tiled=True)]
    ppermute x0 -> x3, waiting for transfers between devices: none -> 39.1 us  [the longest x2 32.6 us: collect(): from_left = lax.ppermute(from_left, axis, upward)]
    psum x1, blocking collectives: 15.6 us -> 41 us  [shards(): lax.psum(jnp.sum(first_scaled * first_normed, axis=0).astype(jnp.bfloat16...]
    dot_general x8, matrix products: 5.85 us -> 22.3 us  [one_block(): jnp.einsum('hqk,hdq->hdk', grad_scores, query_part, preferred_element_typ...]
    while x72 -> x192, local copies, waits for them, and re-layouts: 6.6 us -> 22 us
    dot_general x8, matrix products: 8.64 us -> 21.9 us  [one_block(): jnp.einsum('hqk,hdk->hdq', grad_scores, keys, preferred_element_type=jnp....]
    dot_general x8, matrix products: 17.3 us -> 8.19 us  [one_block(): jnp.einsum('hdq,hdk->hqk', grad_part, values, preferred_element_type=jnp....]
    dynamic_update_slice x20, local copies, waits for them, and re-layouts: 12.2 us -> 21.2 us  [shards(): lax.map(attend_forward, (query_seq, keys_seq, values_seq))]
  transfers between devices with their start and end apart: 3 -> 5, of which waited for: 3 -> 5; matrix products, arithmetic and copies ran while one was open for 2% -> 2% of each run, Pallas kernels for 0% -> 0%
where the time goes in v1:
time: 853 us; the launch traced here: 844 us
  waiting for transfers between devices  287 us (34%)
  matrix products  208 us (24%)
  blocking collectives  146 us (17%)
  local copies, waits for them, and re-layouts  140 us (16%)
  other arithmetic  41 us (5%)
  between operations  15 us (2%)
    reduce_scatter x1, waiting for transfers between devices, shards(): lax.psum_scatter(jnp.dot(output_w, context_low, preferred_element_type=jn...  215 us
    psum x1, blocking collectives, shards(): lax.psum(jnp.sum(first_scaled * first_normed, axis=0).astype(jnp.bfloat16...  41 us
    psum x1, waiting for transfers between devices, shards(): lax.psum((grad_query_w, grad_key_w, grad_value_w, grad_query_b, grad_valu...  33 us
    ppermute x2, waiting for transfers between devices, collect(): from_left = lax.ppermute(from_left, axis, upward)  32.6 us
    dot_general x1, matrix products, shards(): jnp.dot(inner_w, hidden_low, preferred_element_type=jnp.float32)  31.3 us
    unnamed x123, local copies, waits for them, and re-layouts  30.8 us
    dot_general x16, matrix products, one_block(): jnp.einsum('hdq,hdk->hqk', query_part, keys, preferred_element_type=jnp.f...  30 us
    dot_general x6, matrix products, through_weight(): lax.dot_general(weight, grad, (((0,), (0,)), ((), ())), preferred_element...  25.2 us
  transfers between devices with their start and end apart: 5, of which 5 were waited for; matrix products, arithmetic and copies ran while one was open for 2% of the time, Pallas kernels for 0%

profile of v1, /device:TPU:0, one launch (start us, length us, event | category | flops | bytes accessed | tf_op | source)
XLA Modules:
  0.0 844.5 jit_solution(2810689557432233469)
XLA Ops:
  26.4 51.9 %while.58 = (s32[]{:T(128)}, bf16[4,3,64,1024]{3,2,1,0:T(8,128)(2,1)}, f32[4,3,1,1024]{3,2,1,0:T(1,128)}, f32[4,3,1,1024]{3,2,1,0:T(1,128)}, bf16[4,3,64,1024]{3...) while((s32[]{:T(128)}, ...), condition=%wide.region_5.6_spmd, body=%wide.region_0.5_spmd.sunk | while | flops 416805888 | bytes 26758932 | solution.py:165
  28.0 8.6 %while.61 = (s32[]{:T(128)}, bf16[2,3,64,512]{3,2,1,0:T(8,128)(2,1)S(1)}, f32[2,3,1,512]{3,1,2,0:T(4,128)S(1)}, f32[2,3,1,512]{3,1,2,0:T(4,128)S(1)}, bf16[2,3,6...) while((s32[]{:T(128)}, ...), condition=%wide.region_4.4_spmd, body=%wide.region_1.3_spmd.sunk | while | flops 416805888 | bytes 20318304 | solution.py:82
  40.9 8.6 %while.61 = (s32[]{:T(128)}, bf16[2,3,64,512]{3,2,1,0:T(8,128)(2,1)S(1)}, f32[2,3,1,512]{3,1,2,0:T(4,128)S(1)}, f32[2,3,1,512]{3,1,2,0:T(4,128)S(1)}, bf16[2,3,6...) while((s32[]{:T(128)}, ...), condition=%wide.region_4.4_spmd, body=%wide.region_1.3_spmd.sunk | while | flops 416805888 | bytes 20318304 | solution.py:82
  53.8 8.6 %while.61 = (s32[]{:T(128)}, bf16[2,3,64,512]{3,2,1,0:T(8,128)(2,1)S(1)}, f32[2,3,1,512]{3,1,2,0:T(4,128)S(1)}, f32[2,3,1,512]{3,1,2,0:T(4,128)S(1)}, bf16[2,3,6...) while((s32[]{:T(128)}, ...), condition=%wide.region_4.4_spmd, body=%wide.region_1.3_spmd.sunk | while | flops 416805888 | bytes 20318304 | solution.py:82
  66.8 8.6 %while.61 = (s32[]{:T(128)}, bf16[2,3,64,512]{3,2,1,0:T(8,128)(2,1)S(1)}, f32[2,3,1,512]{3,1,2,0:T(4,128)S(1)}, f32[2,3,1,512]{3,1,2,0:T(4,128)S(1)}, bf16[2,3,6...) while((s32[]{:T(128)}, ...), condition=%wide.region_4.4_spmd, body=%wide.region_1.3_spmd.sunk | while | flops 416805888 | bytes 20318304 | solution.py:82
  89.7 12.7 %copy.101 = f32[768,4096]{1,0:T(8,128)} copy(f32[768,4096]{0,1:T(8,128)} %convolution_bitcast_fusion) | data formatting | bytes 25165824
  102.4 214.7 %reduce-scatter.4.cloned.1.call-done = f32[192,4096]{1,0:T(8,128)} async-done(((f32[768,4096]{1,0:T(8,128)}), f32[192,4096]{1,0:T(8,128)}) %reduce-scatter.4.cloned.1.call-update) | async-done | bytes 3145744 | tf_op jit(solution)/shard_map/reduce_scatter | solution.py:167
  320.1 18.6 %psum.161 = f32[4096]{0:T(1024)S(1)} all-reduce(f32[4096]{0:T(1024)S(1)} %get-tuple-element.431), channel_id=1, replica_groups=mesh['dp'=8,'tensor'=4] {'tensor'}, use_global_device_ids=true, to_apply=%region_8.9 | all-reduce | flops 4096 | bytes 32768 | tf_op jit(solution)/shard_map/psum | solution.py:174
  339.1 15.5 %psum.162 = f32[4096]{0:T(1024)S(1)} all-reduce(f32[4096]{0:T(1024)S(1)} %multiply_reduce_fusion.7), channel_id=1, replica_groups=mesh['dp'=8,'tensor'=4] {'tensor'}, use_global_device_ids=true, to_apply=%region_10.11 | all-reduce | flops 4096 | bytes 32768 | tf_op jit(solution)/shard_map/psum | solution.py:176
  354.7 31.3 %fusion.39 = (bf16[768,4096]{0,1:T(8,128)(2,1)S(1)}, f32[768,4096]{0,1:T(8,128)}, f32[4096,768]{1,0:T(8,128)}) fusion(f32[768]{0:T(1024)S(1)} %copy-done.65, bf16[768,192]{0,1:T(8,128)(2,1)S(1)} %copy-done, f32[192,4096]{1,0:T(8,128)S(1)} %get-tuple-element.432, f32[192]{0:T(256)S(1)} %copy-done.67, f32[192]{0:T(256)S(1)} %copy-done.49, ...), kind=kOutput, calls=%fused_computation.74 | convolution fusion | flops 1419509760 | bytes 34935296 | tf_op jit(solution)/shard_map/dot_general | solution.py:181
  390.1 16.4 %psum.163 = f32[4096]{0:T(1024)S(1)} all-reduce(f32[4096]{0:T(1024)S(1)} %get-tuple-element.447), channel_id=1, replica_groups=mesh['dp'=8,'tensor'=4] {'tensor'}, use_global_device_ids=true, to_apply=%region_12.13 | all-reduce | flops 4096 | bytes 32768 | tf_op jit(solution)/shard_map/psum | solution.py:189
  408.8 15.8 %psum.164 = f32[4096]{0:T(1024)S(1)} all-reduce(f32[4096]{0:T(1024)S(1)} %multiply_reduce_fusion.6), channel_id=1, replica_groups=mesh['dp'=8,'tensor'=4] {'tensor'}, use_global_device_ids=true, to_apply=%region_14.15 | all-reduce | flops 4096 | bytes 32768 | tf_op jit(solution)/shard_map/psum | solution.py:191
  430.2 16.3 %all-reduce.3 = (bf16[4096]{0:T(1024)(128)(2,1)S(1)}, bf16[4096]{0:T(1024)(128)(2,1)S(1)}) all-reduce(bf16[4096]{0:T(1024)(128)(2,1)S(1)} %get-tuple-element.331, bf16[4096]{0:T(1024)(128)(2,1)S(1)} %get-tuple-element.335), channel_id=1, replica_groups=mesh['dp'=8,'tensor'=4] {'tensor'}, use_global_device_ids=true, to_apply=%region_18.19 | all-reduce | flops 8192 | bytes 32768 | tf_op jit(solution)/shard_map/psum | solution.py:200
  452.7 13.0 %convert_reduce_fusion = (f32[768]{0:T(1024)}, bf16[768,4096]{0,1:T(8,128)(2,1)S(1)}) fusion(f32[768,4096]{0,1:T(8,128)} %get-tuple-element.430, bf16[192,768]{1,0:T(8,128)(2,1)S(1)} %copy-done.64, f32[192,4096]{1,0:T(8,128)S(1)} %get-tuple-element.426, f32[4096,768]{1,0:T(8,128)} %get-tuple-element.446, f32[768]{0:T(1024)S(1)} %copy-done.65), kind=kOutput, calls=%fused_computation.75 | convolution fusion | flops 1262222592 | bytes 34904064 | tf_op jit(solution)/shard_map/dot_general | solution.py:42
  470.3 41.0 %all-reduce.2 = (bf16[4096]{0:T(1024)(128)(2,1)S(1)}, bf16[4096]{0:T(1024)(128)(2,1)S(1)}) all-reduce(bf16[4096]{0:T(1024)(128)(2,1)S(1)} %get-tuple-element.333, bf16[4096]{0:T(1024)(128)(2,1)S(1)} %get-tuple-element.334), channel_id=1, replica_groups=mesh['dp'=8,'tensor'=4] {'tensor'}, use_global_device_ids=true, to_apply=%region_22.23 | all-reduce | flops 8192 | bytes 32768 | tf_op jit(solution)/shard_map/psum | solution.py:220
  525.1 16.0 %collective-permute-done = bf16[192,4096]{1,0:T(8,128)(2,1)} collective-permute-done((bf16[192,4096]{1,0:T(8,128)(2,1)}, bf16[192,4096]{1,0:T(8,128)(2,1)}, u32[]{:S(2)}, u32[]{:S(2)}) %collective-permute-start) | collective-permute-done | bytes 1572896 | tf_op jit(solution)/shard_map/ppermute | solution.py:23
  557.9 16.7 %collective-permute-done.2 = bf16[192,4096]{1,0:T(8,128)(2,1)S(1)} collective-permute-done((bf16[192,4096]{1,0:T(8,128)(2,1)}, bf16[192,4096]{1,0:T(8,128)(2,1)S(1)}, u32[]{:S(2)}, u32[]{:S(2)}) %collective-permute-start.2) | collective-permute-done | bytes 1572896 | tf_op jit(solution)/shard_map/ppermute | solution.py:23
  585.1 163.0 %while.60 = (s32[]{:T(128)}, bf16[4,3,64,1024]{3,2,1,0:T(8,128)(2,1)}, bf16[4,3,64,1024]{3,2,1,0:T(8,128)(2,1)}, bf16[4,3,64,1024]{3,2,1,0:T(8,128)(2,1)}, bf16[...) while((s32[]{:T(128)}, ...), condition=%wide.region_27.28_spmd, body=%wide.region_23.27_spmd.sunk | while | flops 1021868544 | bytes 141737248 | solution.py:237
  590.7 31.0 %while.62 = (s32[]{:T(128)}, f32[3,64,1024]{2,1,0:T(8,128)}, f32[3,64,1024]{2,1,0:T(8,128)}, bf16[2,3,64,512]{3,2,1,0:T(8,128)(2,1)}, bf16[2,3,64,512]{3,2,1,0:T...) while((s32[]{:T(128)}, f32[3,64,1024]{2,1,0:T(8,128)}, ...), condition=%wide.region_26.26_spmd.clone, body=%wide.region_24.25_spmd.clone.sunk | while | flops 1021868544 | bytes 115685312 | solution.py:120
  631.4 31.0 %while.62 = (s32[]{:T(128)}, f32[3,64,1024]{2,1,0:T(8,128)}, f32[3,64,1024]{2,1,0:T(8,128)}, bf16[2,3,64,512]{3,2,1,0:T(8,128)(2,1)}, bf16[2,3,64,512]{3,2,1,0:T...) while((s32[]{:T(128)}, f32[3,64,1024]{2,1,0:T(8,128)}, ...), condition=%wide.region_26.26_spmd.clone, body=%wide.region_24.25_spmd.clone.sunk | while | flops 1021868544 | bytes 115685312 | solution.py:120
  672.1 31.0 %while.62 = (s32[]{:T(128)}, f32[3,64,1024]{2,1,0:T(8,128)}, f32[3,64,1024]{2,1,0:T(8,128)}, bf16[2,3,64,512]{3,2,1,0:T(8,128)(2,1)}, bf16[2,3,64,512]{3,2,1,0:T...) while((s32[]{:T(128)}, f32[3,64,1024]{2,1,0:T(8,128)}, ...), condition=%wide.region_26.26_spmd.clone, body=%wide.region_24.25_spmd.clone.sunk | while | flops 1021868544 | bytes 115685312 | solution.py:120
  712.8 31.0 %while.62 = (s32[]{:T(128)}, f32[3,64,1024]{2,1,0:T(8,128)}, f32[3,64,1024]{2,1,0:T(8,128)}, bf16[2,3,64,512]{3,2,1,0:T(8,128)(2,1)}, bf16[2,3,64,512]{3,2,1,0:T...) while((s32[]{:T(128)}, f32[3,64,1024]{2,1,0:T(8,128)}, ...), condition=%wide.region_26.26_spmd.clone, body=%wide.region_24.25_spmd.clone.sunk | while | flops 1021868544 | bytes 115685312 | solution.py:120
  765.2 22.7 %all-reduce = (f32[192]{0:T(256)}, f32[192]{0:T(256)}, f32[192]{0:T(256)}, f32[192]{0:T(256)}, f32[192]{0:T(256)}, /*index=5*/f32[768]{0:T(1024)}, f32[192]{0:T(256)}, f32[192]{0:T(256)}, f32[192]{0:T(256)}) all-reduce(f32[192]{0:T(256)S(1)} %reduce_sum.184, f32[192]{0:T(256)S(1)} %reduce_sum.186, ...), channel_id=1, replica_groups=mesh['dp'=8,'tensor'=4] {'dp'}, use_global_device_ids=true, to_apply=%region_32.33 | all-reduce | flops 2304 | bytes 18432 | tf_op jit(solution)/shard_map/psum | solution.py:254
  794.9 33.0 %all-reduce.6.cloned.1.call-done = (f32[192,192]{1,0:T(8,128)}, f32[192,192]{1,0:T(8,128)}, f32[192,192]{1,0:T(8,128)}, f32[768,192]{0,1:T(8,128)}, f32[768,192]{0,1:T(8,128)}, /*index=5*/f32[192,768]{1,0:T(8,128)}) async-done(((f32[192,192]{1,0:T(8,128)}, f32[192,192]{1,0:T(8,128)}, f32[192,192]{1,0:T(8,128)}, f32[768,192]{0,1:T(8,128)}, f32[768,192]{0,1:T(8,128)}, /*index=5*/f32[192,768]{1,0:T(8,128)}), ...) | async-done | bytes 2211856 | tf_op jit(solution)/shard_map/psum | solution.py:254
  (614 shorter events, 343.1 us)
Async XLA Ops:
  7.2 347.5 %copy-start = (bf16[768,192]{0,1:T(8,128)(2,1)S(1)}, bf16[768,192]{0,1:T(8,128)(2,1)}, u32[]{:S(2)}) copy-start(bf16[768,192]{0,1:T(8,128)(2,1)} %param.36) | copy-start | bytes 884740
  7.2 310.0 %reduce-scatter.4.cloned.1.call-start = ((), (), s32[]{:S(2)}) async-start(), calls=%async_computation.1 | async-start | bytes 15728640 | tf_op jit(solution)/shard_map/reduce_scatter | solution.py:167
  102.4 214.8 %copy-start.61 = (f32[192]{0:T(256)S(1)}, f32[192]{0:T(256)}, u32[]{:S(2)}) copy-start(f32[192]{0:T(256)} %param.33) | copy-start | bytes 2308
  102.4 725.5 %all-reduce.6.cloned.1.call-start = ((), (), s32[]{:S(2)}) async-start(), calls=%async_computation.2 | async-start | bytes 4718592 | tf_op jit(solution)/shard_map/psum | solution.py:254
  320.1 199.9 %copy-start.12 = (f32[192,4096]{1,0:T(8,128)}, f32[192,4096]{1,0:T(8,128)S(1)}, u32[]{:S(2)}) copy-start(f32[192,4096]{1,0:T(8,128)S(1)} %get-tuple-element.432) | copy-start | bytes 9437188
  320.1 34.6 %copy-start.49 = (f32[192]{0:T(256)S(1)}, f32[192]{0:T(256)}, u32[]{:S(2)}) copy-start(f32[192]{0:T(256)} %param.34) | copy-start | bytes 2308
  320.1 34.6 %copy-start.65 = (f32[768]{0:T(1024)S(1)}, f32[768]{0:T(1024)}, u32[]{:S(2)}) copy-start(f32[768]{0:T(1024)} %param.37) | copy-start | bytes 9220
  320.1 34.6 %copy-start.67 = (f32[192]{0:T(256)S(1)}, f32[192]{0:T(256)}, u32[]{:S(2)}) copy-start(f32[192]{0:T(256)} %param.35) | copy-start | bytes 2308
  338.8 181.2 %copy-start.34 = (f32[4096]{0:T(1024)}, f32[4096]{0:T(1024)S(1)}, u32[]{:S(2)}) copy-start(f32[4096]{0:T(1024)S(1)} %broadcast_multiply_fusion.1) | copy-start | bytes 49156
  354.7 165.3 %copy-start.37 = (f32[4096]{0:T(1024)}, f32[4096]{0:T(1024)S(1)}, u32[]{:S(2)}) copy-start(f32[4096]{0:T(1024)S(1)} %add_rsqrt_fusion.1) | copy-start | bytes 49156
  354.7 31.3 %copy-start.63 = (bf16[192,768]{1,0:T(8,128)(2,1)S(1)}, bf16[192,768]{1,0:T(8,128)(2,1)}, u32[]{:S(2)}) copy-start(bf16[192,768]{1,0:T(8,128)(2,1)} %param.38) | copy-start | bytes 884740
  354.7 31.3 %copy-start.66 = (f32[192]{0:T(256)S(1)}, f32[192]{0:T(256)}, u32[]{:S(2)}) copy-start(f32[192]{0:T(256)} %param.39) | copy-start | bytes 2308
  390.1 34.5 %copy-start.51 = (f32[192]{0:T(256)S(1)}, f32[192]{0:T(256)}, u32[]{:S(2)}) copy-start(f32[192]{0:T(256)} %param.40) | copy-start | bytes 2308
  516.2 24.9 %collective-permute-start = (bf16[192,4096]{1,0:T(8,128)(2,1)}, bf16[192,4096]{1,0:T(8,128)(2,1)}, u32[]{:S(2)}, u32[]{:S(2)}) collective-permute-start(bf16[192,4096]{1,0:T(8,128)(2,1)} %get-tuple-element.428), channel_id=1, source_target_pairs={{0,1},{1,2},{2,3},{3,0},{4,5},{5,6},{6,7},{7,4},{8,9},{9,10},{10,1... | collective-permute-start | bytes 4718600 | tf_op jit(solution)/shard_map/ppermute | solution.py:23
  516.2 41.6 %collective-permute-start.1 = (bf16[192,4096]{1,0:T(8,128)(2,1)}, bf16[192,4096]{1,0:T(8,128)(2,1)S(1)}, u32[]{:S(2)}, u32[]{:S(2)}) collective-permute-start(bf16[192,4096]{1,0:T(8,128)(2,1)} %get-tuple-element.428), channel_id=1, source_target_pairs={{0,3},{1,0},{2,1},{3,2},{4,7},{5,4},{6,5},{7,6},{8,11},{9,8},{10,9... | collective-permute-start | bytes 4718600 | tf_op jit(solution)/shard_map/ppermute | solution.py:28
  541.1 33.5 %collective-permute-start.2 = (bf16[192,4096]{1,0:T(8,128)(2,1)}, bf16[192,4096]{1,0:T(8,128)(2,1)S(1)}, u32[]{:S(2)}, u32[]{:S(2)}) collective-permute-start(bf16[192,4096]{1,0:T(8,128)(2,1)} %collective-permute-done), channel_id=1, source_target_pairs={{0,1},{1,2},{2,3},{3,0},{4,5},{5,6},{6,7},{7,4},{8,9},{9,10},{10,1... | collective-permute-start | bytes 4718600 | tf_op jit(solution)/shard_map/ppermute | solution.py:23
  762.6 25.3 %copy-start.13 = (f32[192,4096]{1,0:T(8,128)S(1)}, f32[192,4096]{1,0:T(8,128)}, u32[]{:S(2)}) copy-start(f32[192,4096]{1,0:T(8,128)} %copy-done.12) | copy-start | bytes 9437188
  762.6 25.3 %copy-start.35 = (f32[4096]{0:T(1024)S(1)}, f32[4096]{0:T(1024)}, u32[]{:S(2)}) copy-start(f32[4096]{0:T(1024)} %copy-done.34) | copy-start | bytes 49156
  762.6 25.3 %copy-start.38 = (f32[4096]{0:T(1024)S(1)}, f32[4096]{0:T(1024)}, u32[]{:S(2)}) copy-start(f32[4096]{0:T(1024)} %copy-done.37) | copy-start | bytes 49156
  762.6 25.3 %copy-start.40 = (bf16[192,192]{1,0:T(8,128)(2,1)S(1)}, bf16[192,192]{1,0:T(8,128)(2,1)}, u32[]{:S(2)}) copy-start(bf16[192,192]{1,0:T(8,128)(2,1)} %param.27) | copy-start | bytes 221188
  762.7 25.3 %copy-start.46 = (f32[4096]{0:T(1024)S(1)}, f32[4096]{0:T(1024)}, u32[]{:S(2)}) copy-start(f32[4096]{0:T(1024)} %copy-done.45) | copy-start | bytes 49156
  762.7 25.3 %copy-start.48 = (f32[4096]{0:T(1024)S(1)}, f32[4096]{0:T(1024)}, u32[]{:S(2)}) copy-start(f32[4096]{0:T(1024)} %copy-done.47) | copy-start | bytes 49156
  762.7 25.3 %copy-start.50 = (f32[192]{0:T(256)S(1)}, f32[192]{0:T(256)}, u32[]{:S(2)}) copy-start(f32[192]{0:T(256)} %param.34) | copy-start | bytes 2308
  793.1 44.4 %copy-start.1 = (bf16[768,192]{0,1:T(8,128)(2,1)S(1)}, bf16[768,192]{0,1:T(8,128)(2,1)}, u32[]{:S(2)}) copy-start(bf16[768,192]{0,1:T(8,128)(2,1)} %param.36) | copy-start | bytes 884740
  (129 other events, 410.5 us)
Sparse Core Ops, SparseCore 0:
  102.5 214.6 reduce-scatter.3
  765.2 62.6 all-reduce.5
